TPU v7x, 128 devices: a whole 4x4x4 slice. The times are simulated.
128 devices in a mesh: row: 16 (over x_hi, y, core), proto: 8 (over z, x_lo).
Axes of the slice: x: 4 (x_hi: 2, x_lo: 2; x = x_hi * 2 + x_lo), y: 4, z: 4, core: 2. Of those that a mesh axis runs over, the one named last changes fastest.
Arguments:
- tokens: bfloat16 [8192, 4096], P('row'), may hold values from -6 to 6
- w_in: bfloat16 [4096, 8192], P('row', 'proto'), may hold values from -0.09375 to 0.09375
- w_out: bfloat16 [8192, 384], P('proto'), may hold values from -0.0625 to 0.0625
- teacher_z: bfloat16 [8192, 384], P(('row', 'proto')), may hold values from -6 to 6
- proto_student: bfloat16 [384, 49152], P(None, 'proto'), may hold values from -48 to 48
- proto_teacher: bfloat16 [384, 49152], P(None, 'proto'), may hold values from -48 to 48
- center: float32 [49152], P('proto'), may hold values from -0.6 to 0.6
- image_of: int32 [8192], P('row'), may hold values from 0 to 63
Outputs:
- loss: float32 [], replicated
- w_in_grad: float32 [4096, 8192], P('row', 'proto')
- w_out_grad: float32 [8192, 384], P('proto')
- proto_grad: float32 [384, 49152], P('row', 'proto')
All inputs are finite; a program needn't handle non-finite values.
Results may differ from a plain program's by a relative error of at most 0.015.
Values may be sent and summed in bfloat16 or wider, within the bound.
A program may use at most 128 MiB of HBM per device.

v0:
```python
import jax
import jax.numpy as jnp
from jax import lax
from jax.sharding import PartitionSpec as P

tau_teacher = 0.07
tau_student = 0.1
loss_scale = 1048576.0
norm_eps = 1e-06


def gelu_parts(values):
    cumul = 0.5 * (1.0 + jax.scipy.special.erf(values * 0.7071067811865476))
    density = jnp.exp(-0.5 * values * values) * 0.3989422804014327
    return (values * cumul, cumul + values * density)


def inner(left, right):
    return lax.dot_general(
        left, right, (((0,), (0,)), ((), ())), preferred_element_type=jnp.float32
    )


def outer_last(left, right):
    return lax.dot_general(
        left, right, (((1,), (1,)), ((), ())), preferred_element_type=jnp.float32
    )


def normalize(values):
    recip = lax.rsqrt(jnp.sum(values * values, axis=1, keepdims=True) + norm_eps)
    return (recip, values * recip)


def teacher_norm(teacher_z):
    teach = teacher_z.astype(jnp.float32)
    return (teach * lax.rsqrt(jnp.sum(teach * teach, axis=1, keepdims=True) + norm_eps)).astype(
        jnp.bfloat16
    )


def back_norm(dnorm, recip, unit):
    return (recip * (dnorm - unit * jnp.sum(unit * dnorm, axis=1, keepdims=True))).astype(
        jnp.bfloat16
    )


def on_device(tokens, w_in, w_out, teacher_z, proto_student, proto_teacher, center, image_of):
    row_count = tokens.shape[0]
    images = row_count * lax.axis_size("row") // 128
    onehot = (image_of[:, None] == jnp.arange(images, dtype=jnp.int32)[None, :]).astype(jnp.float32)
    counts = lax.psum(jnp.sum(onehot, axis=0), "row")
    weight = 1.0 / (images * jnp.sum(onehot * counts[None, :], axis=1))
    pre = jnp.dot(
        tokens, lax.all_gather(w_in, "row", axis=0, tiled=True), preferred_element_type=jnp.float32
    )
    act, slope = gelu_parts(pre)
    hidden = act.astype(jnp.bfloat16)
    partial_value = jnp.dot(hidden, w_out, preferred_element_type=jnp.float32)
    bott = lax.psum(partial_value, "proto")
    recip, unit = normalize(bott)
    student_n = unit.astype(jnp.bfloat16)
    teacher_n = lax.all_gather(teacher_norm(teacher_z), "proto", axis=0, tiled=True)
    logit_t = (
        jnp.dot(teacher_n, proto_teacher, preferred_element_type=jnp.float32) - center[None, :]
    ) / tau_teacher
    logit_s = jnp.dot(student_n, proto_student, preferred_element_type=jnp.float32) / tau_student
    local_t = jnp.max(logit_t, axis=1)
    local_s = jnp.max(logit_s, axis=1)
    top_t, top_s = lax.pmax((local_t, local_s), "proto")
    exp_t = jnp.exp(logit_t - top_t[:, None])
    exp_s = jnp.exp(logit_s - top_s[:, None])
    total_t, total_s = lax.psum((jnp.sum(exp_t, axis=1), jnp.sum(exp_s, axis=1)), "proto")
    prob_t = exp_t / total_t[:, None]
    prob_s = exp_s / total_s[:, None]
    logp_s = logit_s - top_s[:, None] - jnp.log(total_s)[:, None]
    cross = -jnp.sum(prob_t * logp_s, axis=1)
    loss = lax.psum(jnp.sum(weight * cross), ("row", "proto"))
    grad_s = (loss_scale * weight[:, None] * (prob_s - prob_t) / tau_student).astype(jnp.bfloat16)
    proto_grad = lax.psum_scatter(
        inner(student_n, grad_s).astype(jnp.bfloat16), "row", scatter_dimension=0, tiled=True
    ).astype(jnp.float32)
    dnorm_part = outer_last(grad_s, proto_student)
    dnorm = lax.psum(dnorm_part, "proto")
    dbott = back_norm(dnorm, recip, unit)
    w_out_grad = lax.psum(inner(hidden, dbott).astype(jnp.bfloat16), "row").astype(jnp.float32)
    dpre = (outer_last(dbott, w_out) * slope).astype(jnp.bfloat16)
    w_in_grad = lax.psum_scatter(
        inner(tokens, dpre).astype(jnp.bfloat16), "row", scatter_dimension=0, tiled=True
    ).astype(jnp.float32)
    return (loss, w_in_grad, w_out_grad, proto_grad)


def solution(mesh):
    return jax.shard_map(
        on_device,
        mesh=mesh,
        in_specs=(
            P("row", None),
            P("row", "proto"),
            P("proto", None),
            P(("row", "proto"), None),
            P(None, "proto"),
            P(None, "proto"),
            P("proto"),
            P("row"),
        ),
        out_specs=(P(), P("row", "proto"), P("proto", None), P("row", "proto")),
        check_vma=False,
    )
```

profile of v0, /device:TPU:0, one launch (start us, length us, event | category | flops | bytes accessed | tf_op | source)
XLA Modules:
  0.0 676.0 jit_solution(12270464372114535581)
XLA Ops:
  8.0 0.8 convert_reduce_fusion
  8.8 38.4 %psum.49 = f32[64]{0:T(128)S(1)} all-reduce(f32[64]{0:T(128)S(1)} %convert_reduce_fusion), channel_id=1, replica_groups=mesh['row'=16,'proto'=8] {'row'}, use_global_device_ids=true, to_apply=%region_1.0 | all-reduce | flops 64 | bytes 512 | tf_op jit(solution)/shard_map/psum | solution.py:52
  47.2 0.9 fusion.9
  48.1 0.8 select_reduce_fusion
  48.9 0.9 fusion.10
  49.8 35.8 %all-gather.2.cloned.1.call-done = bf16[4096,1024]{1,0:T(8,128)(2,1)} async-done(((bf16[256,1024]{1,0:T(8,128)(2,1)}), bf16[4096,1024]{1,0:T(8,128)(2,1)}) %all-gather.2.cloned.1.call-update) | async-done | bytes 8388624 | tf_op jit(solution)/shard_map/all_gather | solution.py:55
  85.6 10.6 %multiply_convert_fusion.1 = (bf16[512,1024]{1,0:T(8,128)(2,1)S(1)}, f32[512,1024]{1,0:T(8,128)}) fusion(bf16[512,4096]{1,0:T(8,128)(2,1)} %param.8, bf16[4096,1024]{1,0:T(8,128)(2,1)} %all-gather.2.cloned.1.call-done), kind=kOutput, calls=%fused_computation.19 | convolution fusion | flops 4297588736 | bytes 15728640 | tf_op jit(solution)/shard_map/dot_general | solution.py:54
  96.2 1.6 fusion.14
  97.8 31.3 %all_gather.6 = bf16[512,384]{1,0:T(8,128)(2,1)S(1)} all-gather(bf16[64,384]{1,0:T(8,128)(2,1)S(1)} %fusion.10), channel_id=1, replica_groups=mesh['row'=16,'proto'=8] {'proto'}, dimensions={0}, use_global_device_ids=true | all-gather | bytes 442368 | tf_op jit(solution)/shard_map/all_gather | solution.py:63
  129.1 9.0 %fusion = (f32[512]{0:T(512)S(1)}, f32[512,6144]{1,0:T(8,128)}) fusion(f32[6144]{0:T(1024)S(1)} %copy-done.3, bf16[512,384]{1,0:T(8,128)(2,1)S(1)} %all_gather.6, bf16[384,6144]{1,0:T(8,128)(2,1)} %param.13), kind=kOutput, calls=%fused_computation.7 | convolution fusion | flops 2425355776 | bytes 17721344 | tf_op jit(solution)/shard_map/dot_general | solution.py:65
  138.2 37.0 %all-reduce.6.cloned.1.call-done = f32[512,384]{1,0:T(8,128)} async-done(((f32[512,384]{1,0:T(8,128)}), f32[512,384]{1,0:T(8,128)}) %all-reduce.6.cloned.1.call-update) | async-done | bytes 786448 | tf_op jit(solution)/shard_map/psum | solution.py:60
  175.2 1.3 multiply_reduce_fusion.3
  176.5 10.6 %multiply_reduce_fusion.1 = (f32[512]{0:T(512)S(1)}, f32[512,6144]{1,0:T(8,128)}) fusion(bf16[384,6144]{1,0:T(8,128)(2,1)} %param.12, f32[512,384]{1,0:T(8,128)} %all-reduce.6.cloned.1.call-done, f32[512]{0:T(512)S(1)} %add_rsqrt_fusion), kind=kOutput, calls=%fused_computation.6 | convolution fusion | flops 2422603264 | bytes 18092032 | tf_op jit(solution)/shard_map/dot_general | solution.py:67
  187.1 17.9 %all-reduce.1 = (f32[512]{0:T(512)S(1)}, f32[512]{0:T(512)S(1)}) all-reduce(f32[512]{0:T(512)S(1)} %get-tuple-element.20, f32[512]{0:T(512)S(1)} %get-tuple-element.22), channel_id=1, replica_groups=mesh['row'=16,'proto'=8] {'proto'}, use_global_device_ids=true, to_apply=%region_11.0 | all-reduce | flops 1024 | bytes 8192 | tf_op jit(solution)/shard_map/pmax | solution.py:70
  205.0 10.3 %exponential_reduce_fusion = (f32[512]{0:T(512)S(1)}, f32[512]{0:T(512)S(1)}) fusion(f32[512,6144]{1,0:T(8,128)} %get-tuple-element.21, f32[512]{0:T(512)S(1)} %get-tuple-element.14, f32[512]{0:T(512)S(1)} %get-tuple-element.15, f32[512,6144]{1,0:T(8,128)} %get-tuple-element.23, f32[6144]{0:T(1024)S(1)} %copy-done.3), kind=kLoop, calls=%fused_computation.4 | loop fusion | flops 22019072 | bytes 25198592 | tf_op jit(solution)/shard_map/reduce_sum | solution.py:73
  215.3 16.4 %all-reduce = (f32[512]{0:T(512)S(1)}, f32[512]{0:T(512)S(1)}) all-reduce(f32[512]{0:T(512)S(1)} %get-tuple-element.24, f32[512]{0:T(512)S(1)} %get-tuple-element.25), channel_id=1, replica_groups=mesh['row'=16,'proto'=8] {'proto'}, use_global_device_ids=true, to_apply=%region_13.0 | all-reduce | flops 1024 | bytes 8192 | tf_op jit(solution)/shard_map/psum | solution.py:73
  231.7 12.0 %multiply_convert_fusion = (bf16[512,6144]{1,0:T(8,128)(2,1)S(1)}, f32[512]{0:T(512)S(1)}) fusion(f32[512,6144]{1,0:T(8,128)} %get-tuple-element.21, f32[512]{0:T(512)S(1)} %get-tuple-element.12, f32[512]{0:T(512)S(1)} %broadcast_multiply_fusion, f32[512]{0:T(512)S(1)} %get-tuple-element.14, f32[512]{0:T(512)S(1)} %get-tuple-element.13, ...), kind=kLoop, calls=%fused_computation | loop fusion | flops 44039680 | bytes 31496192 | tf_op jit(solution)/shard_map/convert_element_type | solution.py:79
  243.7 2.7 copy-done.1
  246.3 6.7 fusion.15
  253.1 76.8 %all-reduce.8.cloned.1.call-done = f32[512,384]{1,0:T(8,128)} async-done(((f32[512,384]{1,0:T(8,128)}), f32[512,384]{1,0:T(8,128)}) %all-reduce.8.cloned.1.call-update) | async-done | bytes 786448 | tf_op jit(solution)/shard_map/psum | solution.py:84
  329.9 1.4 multiply_reduce_fusion.2
  331.3 1.3 multiply_convert_fusion.2
  332.6 1.7 convolution_convert_fusion.1
  334.4 7.7 %convolution_convert_fusion = bf16[384,6144]{1,0:T(8,128)(2,1)} fusion(bf16[512,6144]{1,0:T(8,128)(2,1)} %copy-done.1, f32[512,384]{1,0:T(8,128)S(1)} %copy-done.2, f32[512]{0:T(512)S(1)} %add_rsqrt_fusion), kind=kOutput, calls=%fused_computation.10 | convolution fusion | flops 2418671616 | bytes 11798528 | tf_op jit(solution)/shard_map/dot_general | solution.py:19
  342.1 10.4 %convert_bitcast_fusion = bf16[4096,1024]{0,1:T(8,128)(2,1)} fusion(bf16[512,4096]{1,0:T(8,128)(2,1)} %param.8, f32[512,1024]{1,0:T(8,128)} %get-tuple-element.19, bf16[512,384]{1,0:T(8,128)(2,1)S(1)} %multiply_convert_fusion.2, bf16[1024,384]{1,0:T(8,128)(2,1)S(1)} %copy-done), kind=kOutput, calls=%fused_computation.11 | convolution fusion | flops 4707057664 | bytes 15859712 | tf_op jit(solution)/shard_map/dot_general | solution.py:19
  353.1 63.4 %psum.53 = f32[]{:T(128)} all-reduce(f32[]{:T(128)} %multiply_reduce_fusion.4), channel_id=1, replica_groups=mesh['row'=16,'proto'=8] {'row','proto'}, use_global_device_ids=true, to_apply=%region_16.0 | all-reduce | flops 1 | bytes 8 | tf_op jit(solution)/shard_map/psum | solution.py:78
  416.5 57.5 %all-reduce.10.cloned.1.call-done = bf16[1024,384]{1,0:T(8,128)(2,1)} async-done(((bf16[1024,384]{1,0:T(8,128)(2,1)}), bf16[1024,384]{1,0:T(8,128)(2,1)}) %all-reduce.10.cloned.1.call-update) | async-done | bytes 786448 | tf_op jit(solution)/shard_map/psum | solution.py:86
  474.0 2.4 convert_element_type.57
  476.4 85.6 %reduce-scatter.5.cloned.1.call-done = bf16[24,6144]{1,0:T(8,128)(2,1)} async-done(((bf16[384,6144]{1,0:T(8,128)(2,1)}), bf16[24,6144]{1,0:T(8,128)(2,1)}) %reduce-scatter.5.cloned.1.call-update) | async-done | bytes 294928 | tf_op jit(solution)/shard_map/reduce_scatter | solution.py:80
  561.9 1.8 convert_element_type.59
  563.7 103.1 %reduce-scatter.3.cloned.1.call-done = bf16[256,1024]{0,1:T(8,128)(2,1)} async-done(((bf16[4096,1024]{0,1:T(8,128)(2,1)}), bf16[256,1024]{0,1:T(8,128)(2,1)}) %reduce-scatter.3.cloned.1.call-update) | async-done | bytes 524304 | tf_op jit(solution)/shard_map/reduce_scatter | solution.py:88
  666.9 2.2 copy.13
  (24 shorter events, 1.7 us)
Async XLA Ops:
  7.2 89.0 %copy-start = (bf16[1024,384]{1,0:T(8,128)(2,1)S(1)}, bf16[1024,384]{1,0:T(8,128)(2,1)}, u32[]{:S(2)}) copy-start(bf16[1024,384]{1,0:T(8,128)(2,1)} %param.10) | copy-start | bytes 2359300
  7.2 78.4 %all-gather.2.cloned.1.call-start = ((), (), s32[]{:S(2)}) async-start(), calls=%async_computation.2 | async-start | bytes 8912896 | tf_op jit(solution)/shard_map/all_gather | solution.py:55
  7.9 167.3 %all-reduce.6.cloned.1.call-start = ((), (), s32[]{:S(2)}) async-start(), calls=%async_computation.3 | async-start | bytes 1572864 | tf_op jit(solution)/shard_map/psum | solution.py:60
  49.8 79.3 %copy-start.3 = (f32[6144]{0:T(1024)S(1)}, f32[6144]{0:T(1024)}, u32[]{:S(2)}) copy-start(f32[6144]{0:T(1024)} %param.14) | copy-start | bytes 73732
  97.8 232.1 %all-reduce.8.cloned.1.call-start = ((), (), s32[]{:S(2)}) async-start(), calls=%async_computation.4 | async-start | bytes 1572864 | tf_op jit(solution)/shard_map/psum | solution.py:84
  243.7 2.7 copy-start.1
  246.3 83.6 %copy-start.2 = (f32[512,384]{1,0:T(8,128)S(1)}, f32[512,384]{1,0:T(8,128)}, u32[]{:S(2)}) copy-start(f32[512,384]{1,0:T(8,128)} %all-reduce.6.cloned.1.call-done) | copy-start | bytes 2359300
  253.0 220.9 %all-reduce.10.cloned.1.call-start = ((), (), s32[]{:S(2)}) async-start(), calls=%async_computation.6 | async-start | bytes 1572864 | tf_op jit(solution)/shard_map/psum | solution.py:86
  334.3 227.6 %reduce-scatter.5.cloned.1.call-start = ((), (), s32[]{:S(2)}) async-start(), calls=%async_computation.7 | async-start | bytes 5013504 | tf_op jit(solution)/shard_map/reduce_scatter | solution.py:80
  342.1 324.8 %reduce-scatter.3.cloned.1.call-start = ((), (), s32[]{:S(2)}) async-start(), calls=%async_computation.5 | async-start | bytes 8912896 | tf_op jit(solution)/shard_map/reduce_scatter | solution.py:88
Sparse Core Ops, SparseCore 0:
  10.5 75.0 all-gather.1
  97.9 77.2 all-reduce.5
  253.2 76.7 all-reduce.7
  334.4 139.4 all-reduce.9
  477.9 83.9 reduce-scatter.4
  566.0 100.7 reduce-scatter.2
where the time goes:
time: 677 us; the launch traced here: 676 us
  waiting for transfers between devices  397 us (59%)
  blocking collectives  167 us (25%)
  matrix products  58.3 us (9%)
  other arithmetic  34.4 us (5%)
  between operations  14.2 us (2%)
    reduce_scatter x1, waiting for transfers between devices, on_device(): lax.psum_scatter(inner(tokens, dpre).astype(jnp.bfloat16), 'row', scatter...  103 us
    reduce_scatter x1, waiting for transfers between devices, on_device(): lax.psum_scatter(inner(student_n, grad_s).astype(jnp.bfloat16), 'row', sc...  85.6 us
    psum x1, waiting for transfers between devices, on_device(): dnorm = lax.psum(dnorm_part, 'proto')  76.8 us
    psum x1, blocking collectives, on_device(): loss = lax.psum(jnp.sum(weight * cross), ('row', 'proto'))  63.4 us
    psum x1, waiting for transfers between devices, on_device(): lax.psum(inner(hidden, dbott).astype(jnp.bfloat16), 'row')  57.5 us
    psum x1, blocking collectives, on_device(): counts = lax.psum(jnp.sum(onehot, axis=0), 'row')  38.4 us
    psum x1, waiting for transfers between devices, on_device(): bott = lax.psum(partial_value, 'proto')  37 us
    all_gather x1, waiting for transfers between devices, on_device(): lax.all_gather(w_in, 'row', axis=0, tiled=True)  35.8 us
  transfers between devices with their start and end apart: 6, of which 6 were waited for; matrix products, arithmetic and copies ran while one was open for 5% of the time, Pallas kernels for 0%

commit v1 on v0

--- a/solution.py
+++ b/solution.py
@@ -7,6 +7,12 @@
 tau_student = 0.1
 loss_scale = 1048576.0
 norm_eps = 1e-06
+
+
+def update_the_stocks(sheet):
+    arr_next = lax.all_gather(sheet, axis_name="row")
+    plain = jnp.sum(arr_next, axis=0)
+    return plain
 
 
 def gelu_parts(values):
@@ -83,7 +89,7 @@
     dnorm_part = outer_last(grad_s, proto_student)
     dnorm = lax.psum(dnorm_part, "proto")
     dbott = back_norm(dnorm, recip, unit)
-    w_out_grad = lax.psum(inner(hidden, dbott).astype(jnp.bfloat16), "row").astype(jnp.float32)
+    w_out_grad = update_the_stocks(inner(hidden, dbott).astype(jnp.bfloat16)).astype(jnp.float32)
     dpre = (outer_last(dbott, w_out) * slope).astype(jnp.bfloat16)
     w_in_grad = lax.psum_scatter(
         inner(tokens, dpre).astype(jnp.bfloat16), "row", scatter_dimension=0, tiled=True

time: 677 us -> 630 us (0.931)
  waiting for transfers between devices: 397 us -> 335 us
  blocking collectives: 167 us -> 175 us
    all_gather x0 -> x1, waiting for transfers between devices: none -> 89.9 us  [update_the_stocks(): arr_next = lax.all_gather(sheet, axis_name='row')]
    reduce_scatter x1, waiting for transfers between devices: 85.6 us -> 0.01 us  [on_device(): lax.psum_scatter(inner(student_n, grad_s).astype(jnp.bfloat16), 'row', sc...]
    psum x1 -> x0, waiting for transfers between devices: 57.5 us -> none  [on_device(): lax.psum(inner(hidden, dbott).astype(jnp.bfloat16), 'row')]
    psum x1, blocking collectives: 63.4 us -> 71.4 us  [on_device(): loss = lax.psum(jnp.sum(weight * cross), ('row', 'proto'))]
    psum x1, waiting for transfers between devices: 76.8 us -> 69 us  [on_device(): dnorm = lax.psum(dnorm_part, 'proto')]
    reduce_sum x0 -> x1, other arithmetic: none -> 6.83 us  [update_the_stocks(): plain = jnp.sum(arr_next, axis=0)]
  transfers between devices with their start and end apart: 6 -> 6, of which waited for: 6 -> 5; matrix products, arithmetic and copies ran while one was open for 5% -> 6% of each run, Pallas kernels for 0% -> 0%
where the time goes in v1:
time: 630 us; the launch traced here: 628 us
  waiting for transfers between devices  335 us (53%)
  blocking collectives  175 us (28%)
  matrix products  58.4 us (9%)
  other arithmetic  40.1 us (6%)
  between operations  14.2 us (2%)
    reduce_scatter x1, waiting for transfers between devices, on_device(): lax.psum_scatter(inner(tokens, dpre).astype(jnp.bfloat16), 'row', scatter...  103 us
    all_gather x1, waiting for transfers between devices, update_the_stocks(): arr_next = lax.all_gather(sheet, axis_name='row')  89.9 us
    psum x1, blocking collectives, on_device(): loss = lax.psum(jnp.sum(weight * cross), ('row', 'proto'))  71.4 us
    psum x1, waiting for transfers between devices, on_device(): dnorm = lax.psum(dnorm_part, 'proto')  69 us
    psum x1, blocking collectives, on_device(): counts = lax.psum(jnp.sum(onehot, axis=0), 'row')  38.4 us
    psum x1, waiting for transfers between devices, on_device(): bott = lax.psum(partial_value, 'proto')  36.8 us
    all_gather x1, waiting for transfers between devices, on_device(): lax.all_gather(w_in, 'row', axis=0, tiled=True)  35.8 us
    all_gather x1, blocking collectives, on_device(): lax.all_gather(teacher_norm(teacher_z), 'proto', axis=0, tiled=True)  31.3 us
  transfers between devices with their start and end apart: 6, of which 5 were waited for; matrix products, arithmetic and copies ran while one was open for 6% of the time, Pallas kernels for 0%

profile of v1, /device:TPU:0, one launch (start us, length us, event | category | flops | bytes accessed | tf_op | source)
XLA Modules:
  0.0 628.1 jit_solution(10057889930499249779)
XLA Ops:
  8.0 0.8 convert_reduce_fusion
  8.8 38.4 %psum.42 = f32[64]{0:T(128)S(1)} all-reduce(f32[64]{0:T(128)S(1)} %convert_reduce_fusion), channel_id=1, replica_groups=mesh['row'=16,'proto'=8] {'row'}, use_global_device_ids=true, to_apply=%region_1.0 | all-reduce | flops 64 | bytes 512 | tf_op jit(solution)/shard_map/psum | solution.py:58
  47.2 0.9 fusion.9
  48.1 0.8 select_reduce_fusion
  48.9 0.9 fusion.10
  49.8 35.8 %all-gather.4.cloned.1.call-done = bf16[4096,1024]{1,0:T(8,128)(2,1)} async-done(((bf16[256,1024]{1,0:T(8,128)(2,1)}), bf16[4096,1024]{1,0:T(8,128)(2,1)}) %all-gather.4.cloned.1.call-update) | async-done | bytes 8388624 | tf_op jit(solution)/shard_map/all_gather | solution.py:61
  85.6 10.6 %multiply_convert_fusion.1 = (bf16[512,1024]{1,0:T(8,128)(2,1)S(1)}, f32[512,1024]{1,0:T(8,128)}) fusion(bf16[512,4096]{1,0:T(8,128)(2,1)} %param.8, bf16[4096,1024]{1,0:T(8,128)(2,1)} %all-gather.4.cloned.1.call-done), kind=kOutput, calls=%fused_computation.19 | convolution fusion | flops 4297588736 | bytes 15728640 | tf_op jit(solution)/shard_map/dot_general | solution.py:60
  96.2 1.6 fusion.14
  97.8 31.3 %all_gather.12 = bf16[512,384]{1,0:T(8,128)(2,1)S(1)} all-gather(bf16[64,384]{1,0:T(8,128)(2,1)S(1)} %fusion.10), channel_id=1, replica_groups=mesh['row'=16,'proto'=8] {'proto'}, dimensions={0}, use_global_device_ids=true | all-gather | bytes 442368 | tf_op jit(solution)/shard_map/all_gather | solution.py:69
  129.1 9.1 %fusion = (f32[512]{0:T(512)S(1)}, f32[512,6144]{1,0:T(8,128)}) fusion(f32[6144]{0:T(1024)S(1)} %copy-done.3, bf16[512,384]{1,0:T(8,128)(2,1)S(1)} %all_gather.12, bf16[384,6144]{1,0:T(8,128)(2,1)} %param.13), kind=kOutput, calls=%fused_computation.7 | convolution fusion | flops 2425355776 | bytes 17721344 | tf_op jit(solution)/shard_map/dot_general | solution.py:71
  138.2 36.8 %all-reduce.5.cloned.1.call-done = f32[512,384]{1,0:T(8,128)} async-done(((f32[512,384]{1,0:T(8,128)}), f32[512,384]{1,0:T(8,128)}) %all-reduce.5.cloned.1.call-update) | async-done | bytes 786448 | tf_op jit(solution)/shard_map/psum | solution.py:66
  175.0 1.3 multiply_reduce_fusion.3
  176.3 10.7 %multiply_reduce_fusion.1 = (f32[512]{0:T(512)S(1)}, f32[512,6144]{1,0:T(8,128)}) fusion(bf16[384,6144]{1,0:T(8,128)(2,1)} %param.12, f32[512,384]{1,0:T(8,128)} %all-reduce.5.cloned.1.call-done, f32[512]{0:T(512)S(1)} %add_rsqrt_fusion), kind=kOutput, calls=%fused_computation.6 | convolution fusion | flops 2422603264 | bytes 18092032 | tf_op jit(solution)/shard_map/dot_general | solution.py:73
  186.9 17.9 %all-reduce.1 = (f32[512]{0:T(512)S(1)}, f32[512]{0:T(512)S(1)}) all-reduce(f32[512]{0:T(512)S(1)} %get-tuple-element.20, f32[512]{0:T(512)S(1)} %get-tuple-element.22), channel_id=1, replica_groups=mesh['row'=16,'proto'=8] {'proto'}, use_global_device_ids=true, to_apply=%region_11.0 | all-reduce | flops 1024 | bytes 8192 | tf_op jit(solution)/shard_map/pmax | solution.py:76
  204.8 10.3 %exponential_reduce_fusion = (f32[512]{0:T(512)S(1)}, f32[512]{0:T(512)S(1)}) fusion(f32[512,6144]{1,0:T(8,128)} %get-tuple-element.21, f32[512]{0:T(512)S(1)} %get-tuple-element.14, f32[512]{0:T(512)S(1)} %get-tuple-element.15, f32[512,6144]{1,0:T(8,128)} %get-tuple-element.23, f32[6144]{0:T(1024)S(1)} %copy-done.3), kind=kLoop, calls=%fused_computation.4 | loop fusion | flops 22019072 | bytes 25198592 | tf_op jit(solution)/shard_map/reduce_sum | solution.py:79
  215.1 16.4 %all-reduce = (f32[512]{0:T(512)S(1)}, f32[512]{0:T(512)S(1)}) all-reduce(f32[512]{0:T(512)S(1)} %get-tuple-element.24, f32[512]{0:T(512)S(1)} %get-tuple-element.25), channel_id=1, replica_groups=mesh['row'=16,'proto'=8] {'proto'}, use_global_device_ids=true, to_apply=%region_13.0 | all-reduce | flops 1024 | bytes 8192 | tf_op jit(solution)/shard_map/psum | solution.py:79
  231.5 12.0 %multiply_convert_fusion = (bf16[512,6144]{1,0:T(8,128)(2,1)S(1)}, f32[512]{0:T(512)S(1)}) fusion(f32[512,6144]{1,0:T(8,128)} %get-tuple-element.21, f32[512]{0:T(512)S(1)} %get-tuple-element.12, f32[512]{0:T(512)S(1)} %broadcast_multiply_fusion, f32[512]{0:T(512)S(1)} %get-tuple-element.14, f32[512]{0:T(512)S(1)} %get-tuple-element.13, ...), kind=kLoop, calls=%fused_computation | loop fusion | flops 44039680 | bytes 31496192 | tf_op jit(solution)/shard_map/convert_element_type | solution.py:85
  243.5 2.7 copy-done.1
  246.2 6.7 %fusion.15 = f32[512,384]{1,0:T(8,128)} fusion(bf16[512,6144]{1,0:T(8,128)(2,1)S(1)} %get-tuple-element.16, bf16[384,6144]{1,0:T(8,128)(2,1)} %param.12), kind=kOutput, calls=%fused_computation.42 | convolution fusion | flops 2415919104 | bytes 11796480 | tf_op jit(solution)/shard_map/dot_general | solution.py:31
  253.0 7.7 %convolution_convert_fusion = bf16[384,6144]{1,0:T(8,128)(2,1)} fusion(bf16[512,6144]{1,0:T(8,128)(2,1)} %copy-done.1, f32[512,384]{1,0:T(8,128)S(1)} %copy-done.2, f32[512]{0:T(512)S(1)} %add_rsqrt_fusion), kind=kOutput, calls=%fused_computation.10 | convolution fusion | flops 2418671616 | bytes 11798528 | tf_op jit(solution)/shard_map/dot_general | solution.py:25
  260.7 69.0 %all-reduce.7.cloned.1.call-done = f32[512,384]{1,0:T(8,128)} async-done(((f32[512,384]{1,0:T(8,128)}), f32[512,384]{1,0:T(8,128)}) %all-reduce.7.cloned.1.call-update) | async-done | bytes 786448 | tf_op jit(solution)/shard_map/psum | solution.py:90
  329.8 1.4 multiply_reduce_fusion.2
  331.1 1.3 multiply_convert_fusion.2
  332.5 10.4 %convert_bitcast_fusion = bf16[4096,1024]{0,1:T(8,128)(2,1)} fusion(bf16[512,4096]{1,0:T(8,128)(2,1)} %param.8, f32[512,1024]{1,0:T(8,128)} %get-tuple-element.19, bf16[512,384]{1,0:T(8,128)(2,1)S(1)} %multiply_convert_fusion.2, bf16[1024,384]{1,0:T(8,128)(2,1)S(1)} %copy-done), kind=kOutput, calls=%fused_computation.11 | convolution fusion | flops 4707057664 | bytes 15859712 | tf_op jit(solution)/shard_map/dot_general | solution.py:25
  343.0 1.7 convolution_convert_fusion.1
  345.3 71.4 %psum.46 = f32[]{:T(128)} all-reduce(f32[]{:T(128)} %multiply_reduce_fusion.4), channel_id=1, replica_groups=mesh['row'=16,'proto'=8] {'row','proto'}, use_global_device_ids=true, to_apply=%region_16.0 | all-reduce | flops 1 | bytes 8 | tf_op jit(solution)/shard_map/psum | solution.py:84
  416.7 1.8 convert_element_type.61
  418.5 102.6 %reduce-scatter.3.cloned.1.call-done = bf16[256,1024]{0,1:T(8,128)(2,1)} async-done(((bf16[4096,1024]{0,1:T(8,128)(2,1)}), bf16[256,1024]{0,1:T(8,128)(2,1)}) %reduce-scatter.3.cloned.1.call-update) | async-done | bytes 524304 | tf_op jit(solution)/shard_map/reduce_scatter | solution.py:94
  521.1 2.2 copy.13
  523.3 89.9 %all-gather.6.cloned.1.call-done = bf16[16384,384]{1,0:T(8,128)(2,1)} async-done(((bf16[1024,384]{1,0:T(8,128)(2,1)}), bf16[16384,384]{1,0:T(8,128)(2,1)}) %all-gather.6.cloned.1.call-update) | async-done | bytes 12582928 | tf_op jit(solution)/shard_map/all_gather | solution.py:13
  613.2 6.8 %reduce_sum.102 = bf16[1024,384]{1,0:T(8,128)(2,1)S(1)} reduce(bf16[16,1024,384]{2,1,0:T(8,128)(2,1)} %bitcast.18, bf16[]{:T(256)} %constant.31.clone.1), dimensions={0}, to_apply=%region_20.0 | reduce | flops 5898240 | bytes 13369346 | tf_op jit(solution)/shard_map/reduce_sum | solution.py:14
  620.0 1.2 convert_element_type.59
  (25 shorter events, 1.7 us)
Async XLA Ops:
  7.2 89.0 %copy-start = (bf16[1024,384]{1,0:T(8,128)(2,1)S(1)}, bf16[1024,384]{1,0:T(8,128)(2,1)}, u32[]{:S(2)}) copy-start(bf16[1024,384]{1,0:T(8,128)(2,1)} %param.10) | copy-start | bytes 2359300
  7.2 78.4 %all-gather.4.cloned.1.call-start = ((), (), s32[]{:S(2)}) async-start(), calls=%async_computation.2 | async-start | bytes 8912896 | tf_op jit(solution)/shard_map/all_gather | solution.py:61
  7.9 167.1 %all-reduce.5.cloned.1.call-start = ((), (), s32[]{:S(2)}) async-start(), calls=%async_computation.3 | async-start | bytes 1572864 | tf_op jit(solution)/shard_map/psum | solution.py:66
  49.8 79.3 %copy-start.3 = (f32[6144]{0:T(1024)S(1)}, f32[6144]{0:T(1024)}, u32[]{:S(2)}) copy-start(f32[6144]{0:T(1024)} %param.14) | copy-start | bytes 73732
  97.8 232.0 %all-reduce.7.cloned.1.call-start = ((), (), s32[]{:S(2)}) async-start(), calls=%async_computation.4 | async-start | bytes 1572864 | tf_op jit(solution)/shard_map/psum | solution.py:90
  243.4 2.7 copy-start.1
  246.2 6.8 %copy-start.2 = (f32[512,384]{1,0:T(8,128)S(1)}, f32[512,384]{1,0:T(8,128)}, u32[]{:S(2)}) copy-start(f32[512,384]{1,0:T(8,128)} %all-reduce.5.cloned.1.call-done) | copy-start | bytes 2359300
  252.9 163.8 %reduce-scatter.5.cloned.1.call-start = ((), (), s32[]{:S(2)}) async-start(), calls=%async_computation.6 | async-start | bytes 5013504 | tf_op jit(solution)/shard_map/reduce_scatter | solution.py:86
  260.7 260.5 %reduce-scatter.3.cloned.1.call-start = ((), (), s32[]{:S(2)}) async-start(), calls=%async_computation.5 | async-start | bytes 8912896 | tf_op jit(solution)/shard_map/reduce_scatter | solution.py:94
  343.0 270.2 %all-gather.6.cloned.1.call-start = ((), (), s32[]{:S(2)}) async-start(), calls=%async_computation.7 | async-start | bytes 13369344 | tf_op jit(solution)/shard_map/all_gather | solution.py:13
Sparse Core Ops, SparseCore 0:
  10.5 75.0 all-gather.3
  97.9 77.0 all-reduce.4
  253.0 76.7 all-reduce.6
  333.7 82.4 reduce-scatter.4
  420.3 100.7 reduce-scatter.2
  524.0 89.1 all-gather.5
